TPU v7x, 32 devices: a whole 2x2x4 slice. The times are simulated.
32 devices in a mesh: rep: 4 (over x, core), shard: 8 (over z, y).
Axes of the slice: x: 2, y: 2, z: 4, core: 2. Of those that a mesh axis runs over, the one named last changes fastest.
Arguments:
- tokens: bfloat16 [8192, 768], P(('rep', 'shard')), may hold values from -6 to 6
- cotangent: bfloat16 [8192, 768], P(('rep', 'shard')), may hold values from -6 to 6
- offsets: int32 [8192], replicated, may hold values from 0 to 255, as said below
- w_query: bfloat16 [768, 768], P('shard'), may hold values from -0.0546875 to 0.0546875
- w_key: bfloat16 [768, 768], P('shard'), may hold values from -0.21875 to 0.21875
- w_value: bfloat16 [768, 768], P('shard'), may hold values from -0.21875 to 0.21875
- w_attn_out: bfloat16 [768, 768], P('shard'), may hold values from -0.875 to 0.875
- w_gate: bfloat16 [768, 2048], P('shard'), may hold values from -0.21875 to 0.21875
- w_up: bfloat16 [768, 2048], P('shard'), may hold values from -0.21875 to 0.21875
- w_ff_out: bfloat16 [2048, 768], P('shard'), may hold values from -0.125 to 0.125
- gain_attn: bfloat16 [768], P('shard'), may hold values from 0.5 to 1.5
- gain_ff: bfloat16 [768], P('shard'), may hold values from 0.5 to 1.5
- rel_table: bfloat16 [32, 12], P('shard'), may hold values from -4 to 4
Outputs:
- output: bfloat16 [8192, 768], P(('rep', 'shard'))
- d_tokens: float32 [8192, 768], P(('rep', 'shard'))
- d_w_query: float32 [768, 768], P('shard')
- d_w_key: float32 [768, 768], P('shard')
- d_w_value: float32 [768, 768], P('shard')
- d_w_attn_out: float32 [768, 768], P('shard')
- d_w_gate: float32 [768, 2048], P('shard')
- d_w_up: float32 [768, 2048], P('shard')
- d_w_ff_out: float32 [2048, 768], P('shard')
- d_gain_attn: float32 [768], P('shard')
- d_gain_ff: float32 [768], P('shard')
- d_rel_table: float32 [32, 12], P('shard')
Inputs may be any that keep to these rules, and one draw needn't show every extreme that they name: offsets[p] is 0 where a document starts and offsets[p - 1] + 1 otherwise; each sequence of 2048 tokens begins a document; a document lies in one sequence and has 1 to 256 tokens, and some document has exactly 256; every aligned block of 256 tokens holds two or more document starts.
All inputs are finite; a program needn't handle non-finite values.
Results may differ from a plain program's by a relative error of at most 0.014.
The roundings to bfloat16 on the way count: a program that leaves them out, or rounds other values in their place, can miss the bound.
Values may be sent and summed in bfloat16 or wider, within the bound.
No kernel may reach another device: no remote copies, remote signals or barrier semaphores. Data moves between devices by JAX's collectives and lax.ppermute only.
A program may use at most 128 MiB of HBM per device.

v0:
```python
import jax
import jax.numpy as jnp
import numpy as np
from jax import lax
from jax.sharding import PartitionSpec as P

NEG_FILL = -1e30
EPSILON = 1e-06
BORDERS = (1, 2, 3, 4, 5, 6, 7, 8, 12, 16, 23, 32, 46, 64, 91)


def extended(array, sides, width):
    for axis, dim in sides:
        count, length = (lax.axis_size(axis), array.shape[dim])
        up = [(i, (i + 1) % count) for i in range(count - 1)]
        down = [(j, i) for i, j in up]
        last = lax.slice_in_dim(array, length - width, length, axis=dim)
        leading = lax.slice_in_dim(array, 0, width, axis=dim)
        before = lax.ppermute(last, axis, up)
        after = lax.ppermute(leading, axis, down)
        array = jnp.concatenate([before, array, after], axis=dim)
    return array


def from_behind(block, axis, distance):
    devices = range(lax.axis_size(axis))
    route = [(i - distance, i) for i in devices if i - distance in devices]
    return lax.ppermute(block, axis, route)


def bucket_onehot(rows, buckets, sign):
    index = np.arange(4 * rows)
    shifted = np.where(index < 3 * rows, index, index - 4 * rows)
    relative = sign * (shifted - rows)
    distance = np.abs(relative)
    bucket = buckets // 2 * (relative > 0).astype(np.int64)
    for border in BORDERS:
        bucket = bucket + (distance >= border).astype(np.int64)
    return (bucket[:, None] == np.arange(buckets)[None, :]).astype(np.float32)


def rms_norm(values, gain):
    return values * lax.rsqrt(jnp.mean(values * values, axis=-1, keepdims=True) + EPSILON) * gain


def gated_unit(gate, linear):
    return jax.nn.gelu(gate, approximate=True) * linear


def toeplitz(vector, rows):
    period = vector.shape[0]
    tiled = jnp.tile(vector, rows)[: rows * (period - 1)]
    return tiled.reshape(rows, period - 1)[:, : 3 * rows]


def diagonal_sums(matrix, rows):
    period = 4 * rows
    padded = jnp.pad(matrix, ((0, 0), (0, period - 1 - 3 * rows)))
    flat = jnp.pad(padded.reshape(-1), (0, rows))
    return jnp.sum(flat.reshape(rows, period), axis=0)


def split_heads(matrix, heads_count):
    return matrix.reshape(matrix.shape[0], heads_count, -1).transpose(1, 0, 2)


def join_heads(stacked):
    return stacked.transpose(1, 0, 2).reshape(stacked.shape[1], -1)


def per_device(
    tokens,
    cotangent,
    offsets,
    w_query,
    w_key,
    w_value,
    w_attn_out,
    w_gate,
    w_up,
    w_ff_out,
    gain_attn,
    gain_ff,
    rel_table,
):
    rows = tokens.shape[0]
    highest = lax.Precision.HIGHEST
    shard_count = lax.axis_size("shard")
    block_index = lax.axis_index("rep") * shard_count + lax.axis_index("shard")
    starts_all = jnp.arange(offsets.shape[0], dtype=jnp.int32) - offsets
    start_pad = jnp.pad(starts_all, (rows, rows), constant_values=-1)
    start_window = lax.dynamic_slice_in_dim(start_pad, block_index * rows, 3 * rows)
    start_own = start_window[rows : 2 * rows]
    same_doc = start_own[:, None] == start_window[None, :]
    weights = (
        lax.all_gather(w_query, "shard", axis=0, tiled=True),
        lax.all_gather(w_key, "shard", axis=0, tiled=True),
        lax.all_gather(w_value, "shard", axis=0, tiled=True),
        lax.all_gather(w_attn_out, "shard", axis=0, tiled=True),
        lax.all_gather(w_gate, "shard", axis=0, tiled=True),
        lax.all_gather(w_up, "shard", axis=0, tiled=True),
        lax.all_gather(w_ff_out, "shard", axis=0, tiled=True),
        lax.all_gather(gain_attn, "shard", axis=0, tiled=True),
        lax.all_gather(gain_ff, "shard", axis=0, tiled=True),
        lax.all_gather(rel_table, "shard", axis=0, tiled=True),
    )
    (
        query_full,
        key_full,
        value_full,
        attn_out_full,
        gate_full,
        up_full,
        ff_out_full,
        gain_one,
        gain_two,
        table_full,
    ) = weights
    heads_count = table_full.shape[1]
    selector = jnp.asarray(bucket_onehot(rows, table_full.shape[0], 1))
    bias_vecs = jnp.dot(selector, table_full.astype(jnp.float32), precision=highest).T
    layer_in = tokens.astype(jnp.float32)
    normed_one, pull_one = jax.vjp(rms_norm, layer_in, gain_one.astype(jnp.float32))
    normed_low = normed_one.astype(jnp.bfloat16)
    queries = jnp.dot(normed_low, query_full, preferred_element_type=jnp.float32).astype(
        jnp.bfloat16
    )
    key_rows = jnp.dot(normed_low, key_full, preferred_element_type=jnp.float32).astype(
        jnp.bfloat16
    )
    value_rows = jnp.dot(normed_low, value_full, preferred_element_type=jnp.float32).astype(
        jnp.bfloat16
    )
    key_value = extended(jnp.stack([key_rows, value_rows]), (("shard", 1),), rows)
    query_heads = split_heads(queries, heads_count)
    key_heads = split_heads(key_value[0], heads_count)
    value_heads = split_heads(key_value[1], heads_count)

    def head_scores(query_h, key_h, bias_vec):
        scores = jnp.einsum(
            "qd,kd->qk", query_h, key_h, preferred_element_type=jnp.float32
        ) + toeplitz(bias_vec, rows)
        return jnp.where(same_doc, scores, NEG_FILL)

    def head_forward(inputs):
        query_h, key_h, value_h, bias_vec = inputs
        scores = head_scores(query_h, key_h, bias_vec)
        highest_score = jnp.max(scores, axis=-1, keepdims=True)
        expd = jnp.exp(scores - highest_score)
        totals = jnp.sum(expd, axis=-1, keepdims=True)
        probs_low = (expd / totals).astype(jnp.bfloat16)
        mixed = jnp.dot(probs_low, value_h, preferred_element_type=jnp.float32)
        return (mixed, (highest_score + jnp.log(totals))[:, 0])

    mixed, log_totals = lax.map(head_forward, (query_heads, key_heads, value_heads, bias_vecs))
    heads = join_heads(mixed).astype(jnp.bfloat16)
    resid = layer_in + jnp.dot(heads, attn_out_full, preferred_element_type=jnp.float32)
    normed_two, pull_two = jax.vjp(rms_norm, resid, gain_two.astype(jnp.float32))
    normed_ff = normed_two.astype(jnp.bfloat16)
    gate = jnp.dot(normed_ff, gate_full, preferred_element_type=jnp.float32)
    linear = jnp.dot(normed_ff, up_full, preferred_element_type=jnp.float32)
    hidden_full, pull_gate = jax.vjp(gated_unit, gate, linear)
    hidden = hidden_full.astype(jnp.bfloat16)
    output = (resid + jnp.dot(hidden, ff_out_full, preferred_element_type=jnp.float32)).astype(
        jnp.bfloat16
    )
    weights_back = (
        lax.all_gather(w_query, "shard", axis=0, tiled=True),
        lax.all_gather(w_key, "shard", axis=0, tiled=True),
        lax.all_gather(w_value, "shard", axis=0, tiled=True),
        lax.all_gather(w_attn_out, "shard", axis=0, tiled=True),
        lax.all_gather(w_gate, "shard", axis=0, tiled=True),
        lax.all_gather(w_up, "shard", axis=0, tiled=True),
        lax.all_gather(w_ff_out, "shard", axis=0, tiled=True),
        lax.all_gather(gain_attn, "shard", axis=0, tiled=True),
        lax.all_gather(gain_ff, "shard", axis=0, tiled=True),
        lax.all_gather(rel_table, "shard", axis=0, tiled=True),
    )
    query_back, key_back, value_back, attn_out_back, gate_back, up_back, ff_out_back = weights_back[
        :7
    ]
    d_w_ff_out = jnp.einsum("tf,td->fd", hidden, cotangent, preferred_element_type=jnp.float32)
    d_hidden = jnp.einsum("td,fd->tf", cotangent, ff_out_back, preferred_element_type=jnp.float32)
    d_gate_full, d_linear_full = pull_gate(d_hidden)
    d_gate = d_gate_full.astype(jnp.bfloat16)
    d_linear = d_linear_full.astype(jnp.bfloat16)
    d_w_gate = jnp.einsum("td,tf->df", normed_ff, d_gate, preferred_element_type=jnp.float32)
    d_w_up = jnp.einsum("td,tf->df", normed_ff, d_linear, preferred_element_type=jnp.float32)
    d_normed_ff = jnp.einsum("tf,df->td", d_gate, gate_back, preferred_element_type=jnp.float32)
    d_normed_ff = d_normed_ff + jnp.einsum(
        "tf,df->td", d_linear, up_back, preferred_element_type=jnp.float32
    )
    d_resid_norm, d_gain_two = pull_two(d_normed_ff)
    d_resid = cotangent.astype(jnp.float32) + d_resid_norm
    d_attn = d_resid.astype(jnp.bfloat16)
    d_w_attn_out = jnp.einsum("th,td->hd", heads, d_attn, preferred_element_type=jnp.float32)
    d_heads = jnp.einsum(
        "td,hd->th", d_attn, attn_out_back, preferred_element_type=jnp.float32
    ).astype(jnp.bfloat16)
    d_head_split = split_heads(d_heads, heads_count)

    def query_side(query_h, key_h, value_h, bias_vec, grad_out, log_total):
        scores = head_scores(query_h, key_h, bias_vec)
        probs = jnp.exp(scores - log_total[:, None])
        d_probs = jnp.einsum("qd,kd->qk", grad_out, value_h, preferred_element_type=jnp.float32)
        weighted = jnp.sum(d_probs * probs, axis=-1, keepdims=True)
        d_scores = (probs * (d_probs - weighted)).astype(jnp.bfloat16)
        return (probs, d_scores, weighted)

    def head_backward(inputs):
        query_h, key_h, value_h, bias_vec, grad_out, log_total = inputs
        probs, d_scores, weighted = query_side(
            query_h, key_h, value_h, bias_vec, grad_out, log_total
        )
        probs_low = probs.astype(jnp.bfloat16)
        d_query_h = jnp.einsum("qk,kd->qd", d_scores, key_h, preferred_element_type=jnp.float32)
        d_key_h = jnp.einsum("qk,qd->kd", d_scores, query_h, preferred_element_type=jnp.float32)
        d_value_h = jnp.einsum("qk,qd->kd", probs_low, grad_out, preferred_element_type=jnp.float32)
        d_bias = diagonal_sums(d_scores.astype(jnp.float32), rows)
        return (d_query_h, d_key_h, d_value_h, d_bias)

    d_query_split, d_key_split, d_value_split, d_bias_vecs = lax.map(
        head_backward, (query_heads, key_heads, value_heads, bias_vecs, d_head_split, log_totals)
    )
    d_queries = join_heads(d_query_split).astype(jnp.bfloat16)
    d_key_value = jnp.stack([join_heads(d_key_split), join_heads(d_value_split)])
    from_next = from_behind(d_key_value[:, :rows].astype(jnp.bfloat16), "shard", -1).astype(
        jnp.float32
    )
    from_prev = from_behind(d_key_value[:, 2 * rows :].astype(jnp.bfloat16), "shard", 1).astype(
        jnp.float32
    )
    d_own = (d_key_value[:, rows : 2 * rows] + from_next + from_prev).astype(jnp.bfloat16)
    d_keys = d_own[0]
    d_values = d_own[1]
    d_w_query = jnp.einsum("td,th->dh", normed_low, d_queries, preferred_element_type=jnp.float32)
    d_w_key = jnp.einsum("td,th->dh", normed_low, d_keys, preferred_element_type=jnp.float32)
    d_w_value = jnp.einsum("td,th->dh", normed_low, d_values, preferred_element_type=jnp.float32)
    d_normed = jnp.einsum("th,dh->td", d_queries, query_back, preferred_element_type=jnp.float32)
    d_normed = d_normed + jnp.einsum(
        "th,dh->td", d_keys, key_back, preferred_element_type=jnp.float32
    )
    d_normed = d_normed + jnp.einsum(
        "th,dh->td", d_values, value_back, preferred_element_type=jnp.float32
    )
    d_layer_norm, d_gain_one = pull_one(d_normed)
    d_tokens = d_resid + d_layer_norm
    d_table = jnp.dot(selector.T, d_bias_vecs.T, precision=highest)
    local = (
        lax.psum_scatter(d_w_query, "shard", scatter_dimension=0, tiled=True),
        lax.psum_scatter(d_w_key, "shard", scatter_dimension=0, tiled=True),
        lax.psum_scatter(d_w_value, "shard", scatter_dimension=0, tiled=True),
        lax.psum_scatter(d_w_attn_out, "shard", scatter_dimension=0, tiled=True),
        lax.psum_scatter(d_w_gate, "shard", scatter_dimension=0, tiled=True),
        lax.psum_scatter(d_w_up, "shard", scatter_dimension=0, tiled=True),
        lax.psum_scatter(d_w_ff_out, "shard", scatter_dimension=0, tiled=True),
        lax.psum_scatter(d_gain_one, "shard", scatter_dimension=0, tiled=True),
        lax.psum_scatter(d_gain_two, "shard", scatter_dimension=0, tiled=True),
        lax.psum_scatter(d_table, "shard", scatter_dimension=0, tiled=True),
    )
    summed = lax.psum(
        (
            local[0],
            local[1],
            local[2],
            local[3],
            local[4],
            local[5],
            local[6],
            local[7],
            local[8],
            local[9],
        ),
        "rep",
    )
    return (
        output,
        d_tokens,
        summed[0],
        summed[1],
        summed[2],
        summed[3],
        summed[4],
        summed[5],
        summed[6],
        summed[7],
        summed[8],
        summed[9],
    )


def solution(mesh):
    return jax.shard_map(
        per_device,
        mesh=mesh,
        in_specs=(
            P(("rep", "shard"), None),
            P(("rep", "shard"), None),
            P(),
            P("shard", None),
            P("shard", None),
            P("shard", None),
            P("shard", None),
            P("shard", None),
            P("shard", None),
            P("shard", None),
            P("shard"),
            P("shard"),
            P("shard", None),
        ),
        out_specs=(
            P(("rep", "shard"), None),
            P(("rep", "shard"), None),
            P("shard", None),
            P("shard", None),
            P("shard", None),
            P("shard", None),
            P("shard", None),
            P("shard", None),
            P("shard", None),
            P("shard"),
            P("shard"),
            P("shard", None),
        ),
        check_vma=False,
    )
```

profile of v0, /device:TPU:0, one launch (start us, length us, event | category | flops | bytes accessed | tf_op | source)
XLA Modules:
  0.0 1214.5 jit_solution(13365985797929775624)
XLA Ops:
  15.7 23.1 %all-reduce.11 = (bf16[768]{0:T(1024)(128)(2,1)S(1)}, bf16[768]{0:T(1024)(128)(2,1)S(1)}) all-reduce(bf16[768]{0:T(1024)(128)(2,1)S(1)} %dynamic-update-slice, bf16[768]{0:T(1024)(128)(2,1)S(1)} %dynamic-update-slice.1), channel_id=1, replica_groups=mesh['rep'=4,'shard'=8] {'shard'}, use_global_device_ids=true, to_apply=%add.3 | all-reduce | flops 1536 | bytes 6144
  40.0 13.9 %all-gather.11.cloned.1.call-done = bf16[768,768]{1,0:T(8,128)(2,1)} async-done(((bf16[96,768]{1,0:T(8,128)(2,1)}), bf16[768,768]{1,0:T(8,128)(2,1)}) %all-gather.11.cloned.1.call-update) | async-done | bytes 1179664 | tf_op jit(solution)/shard_map/all_gather | solution.py:97
  55.9 40.1 %all-gather.13.cloned.1.call-done = bf16[768,768]{1,0:T(8,128)(2,1)} async-done(((bf16[96,768]{1,0:T(8,128)(2,1)}), bf16[768,768]{1,0:T(8,128)(2,1)}) %all-gather.13.cloned.1.call-update) | async-done | bytes 1179664 | tf_op jit(solution)/shard_map/all_gather | solution.py:98
  102.6 44.6 %all-gather = bf16[8,4,12]{2,1,0:T(4,128)(2,1)S(1)} all-gather(bf16[1,4,12]{2,1,0:T(4,128)(2,1)S(1)} %bitcast.220), channel_id=1, replica_groups=mesh['rep'=4,'shard'=8] {'shard'}, dimensions={0}, use_global_device_ids=true | all-gather | bytes 864 | tf_op jit(solution)/shard_map/all_gather | solution.py:105
  147.6 6.3 all-gather.9.cloned.1.call-done
  167.9 55.0 %while.32 = (s32[]{:T(128)}, bf16[12,256,64]{1,2,0:T(8,128)(2,1)}, f32[12,256]{1,0:T(8,128)S(1)}, bf16[12,256,64]{2,1,0:T(8,128)(2,1)}, bf16[12,768,64]{2,1,0:T(...) while((s32[]{:T(128)}, bf16[12,256,64]{1,2,0:T(8,128)(2,1)}, ...), condition=%wide.region_4.5_spmd.clone, body=%wide.region_1.4_spmd.clone.sunk | while | flops 52100864 | bytes 8939637 | solution.py:155
  225.1 32.0 %all-gather.17.cloned.1.call-done = bf16[768,2048]{1,0:T(8,128)(2,1)} async-done(((bf16[96,2048]{1,0:T(8,128)(2,1)}), bf16[768,2048]{1,0:T(8,128)(2,1)}) %all-gather.17.cloned.1.call-update) | async-done | bytes 3145744 | tf_op jit(solution)/shard_map/all_gather | solution.py:100
  260.0 58.3 %all-gather.19.cloned.1.call-done = bf16[768,2048]{1,0:T(8,128)(2,1)} async-done(((bf16[96,2048]{1,0:T(8,128)(2,1)}), bf16[768,2048]{1,0:T(8,128)(2,1)}) %all-gather.19.cloned.1.call-update) | async-done | bytes 3145744 | tf_op jit(solution)/shard_map/all_gather | solution.py:101
  318.3 4.2 fusion.86
  322.5 57.1 %all-gather.21.cloned.1.call-done = bf16[2048,768]{1,0:T(8,128)(2,1)} async-done(((bf16[256,768]{1,0:T(8,128)(2,1)}), bf16[2048,768]{1,0:T(8,128)(2,1)}) %all-gather.21.cloned.1.call-update) | async-done | bytes 3145744 | tf_op jit(solution)/shard_map/all_gather | solution.py:102
  379.6 5.9 multiply_convert_fusion.1
  394.1 129.4 %while.33 = (s32[]{:T(128)}, bf16[12,256,64]{1,2,0:T(8,128)(2,1)}, f32[12,768,64]{1,2,0:T(8,128)}, f32[12,768,64]{1,2,0:T(8,128)}, f32[12,1024]{1,0:T(8,128)}, /...) while((s32[]{:T(128)}, bf16[12,256,64]{1,2,0:T(8,128)(2,1)}, ...), condition=%wide.region_10.11_spmd.clone, body=%wide.region_7.10_spmd.clone.sunk | while | flops 128318208 | bytes 23038184 | solution.py:222
  530.6 4.7 collective-permute-start.3
  535.4 17.4 %collective-permute-done.2 = bf16[2,256,768]{1,2,0:T(8,128)(2,1)S(1)} collective-permute-done((bf16[2,256,768]{1,2,0:T(8,128)(2,1)S(1)}, bf16[2,256,768]{1,2,0:T(8,128)(2,1)S(1)}, u32[]{:S(2)}, u32[]{:S(2)}) %collective-permute-start.2) | collective-permute-done | bytes 786464 | tf_op jit(solution)/shard_map/ppermute | solution.py:28
  552.8 19.0 %collective-permute-done.3 = bf16[2,256,768]{1,2,0:T(8,128)(2,1)S(1)} collective-permute-done((bf16[2,256,768]{1,2,0:T(8,128)(2,1)S(1)}, bf16[2,256,768]{1,2,0:T(8,128)(2,1)S(1)}, u32[]{:S(2)}, u32[]{:S(2)}) %collective-permute-start.3) | collective-permute-done | bytes 786464 | tf_op jit(solution)/shard_map/ppermute | solution.py:28
  593.3 22.5 %reduce-scatter.8.cloned.1.call-done = f32[96,768]{1,0:T(8,128)} async-done(((f32[768,768]{1,0:T(8,128)}), f32[96,768]{1,0:T(8,128)}) %reduce-scatter.8.cloned.1.call-update) | async-done | bytes 294928 | tf_op jit(solution)/shard_map/reduce_scatter | solution.py:250
  615.7 71.4 %reduce-scatter.10.cloned.1.call-done = f32[96,768]{1,0:T(8,128)} async-done(((f32[768,768]{1,0:T(8,128)}), f32[96,768]{1,0:T(8,128)}) %reduce-scatter.10.cloned.1.call-update) | async-done | bytes 294928 | tf_op jit(solution)/shard_map/reduce_scatter | solution.py:251
  687.2 71.6 %reduce-scatter.12.cloned.1.call-done = f32[96,768]{1,0:T(8,128)} async-done(((f32[768,768]{1,0:T(8,128)}), f32[96,768]{1,0:T(8,128)}) %reduce-scatter.12.cloned.1.call-update) | async-done | bytes 294928 | tf_op jit(solution)/shard_map/reduce_scatter | solution.py:252
  758.7 120.5 %reduce-scatter.16.cloned.1.call-done = f32[96,2048]{1,0:T(8,128)} async-done(((f32[768,2048]{1,0:T(8,128)}), f32[96,2048]{1,0:T(8,128)}) %reduce-scatter.16.cloned.1.call-update) | async-done | bytes 786448 | tf_op jit(solution)/shard_map/reduce_scatter | solution.py:254
  879.2 120.7 %reduce-scatter.18.cloned.1.call-done = f32[96,2048]{1,0:T(8,128)} async-done(((f32[768,2048]{1,0:T(8,128)}), f32[96,2048]{1,0:T(8,128)}) %reduce-scatter.18.cloned.1.call-update) | async-done | bytes 786448 | tf_op jit(solution)/shard_map/reduce_scatter | solution.py:255
  999.9 120.5 %reduce-scatter.20.cloned.1.call-done = f32[256,768]{1,0:T(8,128)} async-done(((f32[2048,768]{1,0:T(8,128)}), f32[256,768]{1,0:T(8,128)}) %reduce-scatter.20.cloned.1.call-update) | async-done | bytes 786448 | tf_op jit(solution)/shard_map/reduce_scatter | solution.py:256
  1128.6 35.3 %all-reduce.8 = (f32[768]{0:T(1024)S(1)}, f32[768]{0:T(1024)S(1)}, f32[32,12]{1,0:T(8,128)S(1)}) all-reduce(f32[768]{0:T(1024)S(1)} %get-tuple-element.333, f32[768]{0:T(1024)S(1)} %get-tuple-element.331, f32[32,12]{1,0:T(8,128)} %fusion.92), channel_id=9, replica_groups=mesh['rep'=4,'shard'=8] {'shard'}, use_global_device_ids=true, to_apply=%region_27.28.clone | all-reduce | flops 1920 | bytes 15360
  1164.0 6.2 all-reduce.9
  1172.1 26.3 %all-reduce.14.cloned.1.call-done = (f32[96,768]{1,0:T(8,128)}, f32[96,768]{1,0:T(8,128)}, f32[96,768]{1,0:T(8,128)}, f32[96,768]{1,0:T(8,128)}, f32[96,2048]{1,...) async-done(((f32[96,768]{1,0:T(8,128)}, f32[96,768]{1,0:T(8,128)}, f32[96,768]{1,0:T(8,128)}, f32[96,768]{1,0:T(8,128)}, f32[96,2048]{1,0:T(8,128)}, ...) | async-done | bytes 3538960 | tf_op jit(solution)/shard_map/psum | solution.py:261
  (531 shorter events, 274.9 us)
Async XLA Ops:
  7.2 46.7 %all-gather.11.cloned.1.call-start = ((), (), s32[]{:S(2)}) async-start(), calls=%async_computation.8 | async-start | bytes 1327104 | tf_op jit(solution)/shard_map/all_gather | solution.py:97
  7.9 88.0 %all-gather.13.cloned.1.call-start = ((), (), s32[]{:S(2)}) async-start(), calls=%async_computation.9 | async-start | bytes 1327104 | tf_op jit(solution)/shard_map/all_gather | solution.py:98
  8.7 145.2 %all-gather.9.cloned.1.call-start = ((), (), s32[]{:S(2)}) async-start(), calls=%async_computation.7 | async-start | bytes 1327104 | tf_op jit(solution)/shard_map/all_gather | solution.py:96
  9.4 213.6 %all-gather.15.cloned.1.call-start = ((), (), s32[]{:S(2)}) async-start(), calls=%async_computation.10 | async-start | bytes 1327104 | tf_op jit(solution)/shard_map/all_gather | solution.py:99
  10.0 247.2 %all-gather.17.cloned.1.call-start = ((), (), s32[]{:S(2)}) async-start(), calls=%async_computation.11 | async-start | bytes 3538944 | tf_op jit(solution)/shard_map/all_gather | solution.py:100
  10.6 307.7 %all-gather.19.cloned.1.call-start = ((), (), s32[]{:S(2)}) async-start(), calls=%async_computation.12 | async-start | bytes 3538944 | tf_op jit(solution)/shard_map/all_gather | solution.py:101
  11.1 368.5 %all-gather.21.cloned.1.call-start = ((), (), s32[]{:S(2)}) async-start(), calls=%async_computation.13 | async-start | bytes 3538944 | tf_op jit(solution)/shard_map/all_gather | solution.py:102
  11.9 581.4 %reduce-scatter.14.cloned.1.call-start = ((), (), s32[]{:S(2)}) async-start(), calls=%async_computation.17 | async-start | bytes 2654208 | tf_op jit(solution)/shard_map/reduce_scatter | solution.py:253
  98.7 60.1 %collective-permute-start = (bf16[2,256,768]{2,1,0:T(8,128)(2,1)}, bf16[2,256,768]{2,1,0:T(8,128)(2,1)S(1)}, u32[]{:S(2)}, u32[]{:S(2)}) collective-permute-start(bf16[2,256,768]{2,1,0:T(8,128)(2,1)} %pad_maximum_fusion.2), channel_id=1, source_target_pairs={{0,1},{1,2},{2,3},{3,4},{4,5},{5,6},{6,7},{8,9},{9,10},{10,11},{11... | collective-permute-start | bytes 2359304 | tf_op jit(solution)/shard_map/ppermute | solution.py:19
  101.2 57.6 %collective-permute-start.1 = (bf16[2,256,768]{2,1,0:T(8,128)(2,1)}, bf16[2,256,768]{2,1,0:T(8,128)(2,1)S(1)}, u32[]{:S(2)}, u32[]{:S(2)}) collective-permute-start(bf16[2,256,768]{2,1,0:T(8,128)(2,1)} %pad_maximum_fusion.2), channel_id=1, source_target_pairs={{1,0},{2,1},{3,2},{4,3},{5,4},{6,5},{7,6},{9,8},{10,9},{11,10},{12... | collective-permute-start | bytes 2359304 | tf_op jit(solution)/shard_map/ppermute | solution.py:20
  225.0 164.5 %copy-start.7 = (f32[256,768]{1,0:T(8,128)}, f32[256,768]{1,0:T(8,128)S(1)}, u32[]{:S(2)}) copy-start(f32[256,768]{1,0:T(8,128)S(1)} %get-tuple-element.408) | copy-start | bytes 2359300
  225.1 93.2 %copy-start.2 = (bf16[256,768]{1,0:T(8,128)(2,1)}, bf16[256,768]{1,0:T(8,128)(2,1)S(1)}, u32[]{:S(2)}) copy-start(bf16[256,768]{1,0:T(8,128)(2,1)S(1)} %multiply_convert_fusion.3) | copy-start | bytes 1179652
  393.1 222.6 %reduce-scatter.8.cloned.1.call-start = ((), (), s32[]{:S(2)}) async-start(), calls=%async_computation.14 | async-start | bytes 2654208 | tf_op jit(solution)/shard_map/reduce_scatter | solution.py:250
  526.9 160.2 %reduce-scatter.10.cloned.1.call-start = ((), (), s32[]{:S(2)}) async-start(), calls=%async_computation.15 | async-start | bytes 2654208 | tf_op jit(solution)/shard_map/reduce_scatter | solution.py:251
  529.2 23.6 %collective-permute-start.2 = (bf16[2,256,768]{1,2,0:T(8,128)(2,1)S(1)}, bf16[2,256,768]{1,2,0:T(8,128)(2,1)S(1)}, u32[]{:S(2)}, u32[]{:S(2)}) collective-permute-start(bf16[2,256,768]{1,2,0:T(8,128)(2,1)S(1)} %get-tuple-element.401), channel_id=1, source_target_pairs={{1,0},{2,1},{3,2},{4,3},{5,4},{6,5},{7,6},{9,8},{10,9},{11,10},{12... | collective-permute-start | bytes 2359304 | tf_op jit(solution)/shard_map/ppermute | solution.py:28
  530.6 41.1 %collective-permute-start.3 = (bf16[2,256,768]{1,2,0:T(8,128)(2,1)S(1)}, bf16[2,256,768]{1,2,0:T(8,128)(2,1)S(1)}, u32[]{:S(2)}, u32[]{:S(2)}) collective-permute-start(bf16[2,256,768]{1,2,0:T(8,128)(2,1)S(1)} %get-tuple-element.402), channel_id=1, source_target_pairs={{0,1},{1,2},{2,3},{3,4},{4,5},{5,6},{6,7},{8,9},{9,10},{10,11},{11... | collective-permute-start | bytes 2359304 | tf_op jit(solution)/shard_map/ppermute | solution.py:28
  574.1 184.6 %reduce-scatter.12.cloned.1.call-start = ((), (), s32[]{:S(2)}) async-start(), calls=%async_computation.16 | async-start | bytes 2654208 | tf_op jit(solution)/shard_map/reduce_scatter | solution.py:252
  576.2 303.0 %reduce-scatter.16.cloned.1.call-start = ((), (), s32[]{:S(2)}) async-start(), calls=%async_computation.18 | async-start | bytes 7077888 | tf_op jit(solution)/shard_map/reduce_scatter | solution.py:254
  580.0 419.9 %reduce-scatter.18.cloned.1.call-start = ((), (), s32[]{:S(2)}) async-start(), calls=%async_computation.19 | async-start | bytes 7077888 | tf_op jit(solution)/shard_map/reduce_scatter | solution.py:255
  584.8 535.6 %reduce-scatter.20.cloned.1.call-start = ((), (), s32[]{:S(2)}) async-start(), calls=%async_computation.20 | async-start | bytes 7077888 | tf_op jit(solution)/shard_map/reduce_scatter | solution.py:256
  589.8 608.6 %all-reduce.14.cloned.1.call-start = ((), (), s32[]{:S(2)}) async-start(), calls=%async_computation.21 | async-start | bytes 7077888 | tf_op jit(solution)/shard_map/psum | solution.py:261
  593.2 527.3 %copy-start.19 = (f32[1024,32]{1,0:T(8,128)S(1)}, f32[1024,32]{1,0:T(8,128)}, u32[]{:S(2)}) copy-start(f32[1024,32]{1,0:T(8,128)} %constant.112.clone) | copy-start | bytes 393220
  593.2 527.3 %copy-start.31 = (f32[12,1024]{1,0:T(8,128)S(1)}, f32[12,1024]{1,0:T(8,128)}, u32[]{:S(2)}) copy-start(f32[12,1024]{1,0:T(8,128)} %get-tuple-element.212) | copy-start | bytes 147460
  593.2 528.8 %copy-start.8 = (f32[256,768]{1,0:T(8,128)S(1)}, f32[256,768]{1,0:T(8,128)}, u32[]{:S(2)}) copy-start(f32[256,768]{1,0:T(8,128)} %copy-done.7) | copy-start | bytes 2359300
  (52 other events, 561.7 us)
Sparse Core Ops, SparseCore 0:
  10.2 43.6 all-gather.10
  56.1 39.8 all-gather.12
  98.2 55.7 all-gather.8
  155.9 39.8 all-gather.14
  197.9 59.2 all-gather.16
  259.2 59.0 all-gather.18
  320.5 59.0 all-gather.20
  393.2 67.7 reduce-scatter.13
  527.1 88.6 reduce-scatter.7
  619.1 68.0 reduce-scatter.9
  690.7 68.0 reduce-scatter.11
  762.2 116.9 reduce-scatter.15
  882.8 117.0 reduce-scatter.17
  1003.3 117.0 reduce-scatter.19
  1123.1 75.1 all-reduce.13
where the time goes:
time: 1220 us; the launch traced here: 1210 us
  waiting for transfers between devices  802 us (66%)
  matrix products  178 us (15%)
  blocking collectives  109 us (9%)
  local copies, waits for them, and re-layouts  82.9 us (7%)
  between operations  16.4 us (1%)
  other arithmetic  13.6 us (1%)
    reduce_scatter x1, waiting for transfers between devices, per_device(): lax.psum_scatter(d_w_up, 'shard', scatter_dimension=0, tiled=True)  121 us
    reduce_scatter x1, waiting for transfers between devices, per_device(): lax.psum_scatter(d_w_ff_out, 'shard', scatter_dimension=0, tiled=True)  121 us
    reduce_scatter x1, waiting for transfers between devices, per_device(): lax.psum_scatter(d_w_gate, 'shard', scatter_dimension=0, tiled=True)  120 us
    reduce_scatter x1, waiting for transfers between devices, per_device(): lax.psum_scatter(d_w_value, 'shard', scatter_dimension=0, tiled=True)  71.6 us
    reduce_scatter x1, waiting for transfers between devices, per_device(): lax.psum_scatter(d_w_key, 'shard', scatter_dimension=0, tiled=True)  71.4 us
    unnamed x2, blocking collectives  58.4 us
    all_gather x1, waiting for transfers between devices, per_device(): lax.all_gather(w_up, 'shard', axis=0, tiled=True)  58.3 us
    all_gather x1, waiting for transfers between devices, per_device(): lax.all_gather(w_ff_out, 'shard', axis=0, tiled=True)  57.1 us
  transfers between devices with their start and end apart: 19, of which 15 were waited for; matrix products, arithmetic and copies ran while one was open for 20% of the time, Pallas kernels for 0%

commit v1 on v0

v1 whole, which is shorter than its diff:
```python
import functools

import jax
import jax.numpy as jnp
import numpy as np
from jax import lax
from jax.experimental import pallas as pl
from jax.experimental.pallas import tpu as pltpu
from jax.sharding import PartitionSpec as P

NEG_FILL = -1e30
EPSILON = 1e-06
BORDERS = (1, 2, 3, 4, 5, 6, 7, 8, 12, 16, 23, 32, 46, 64, 91)
LANES = 128
PARTS = 4
GROUPS = (8, 4)
LOW = jnp.bfloat16
FULL = jnp.float32
GELU_A = float(np.sqrt(2.0 / np.pi))
GELU_B = 0.044715


def bits_of(count):
    return count.bit_length() - 1


def swap(block, axis, bit):
    count = lax.axis_size(axis)
    return lax.ppermute(block, axis, [(i, i ^ (1 << bit)) for i in range(count)])


def add_low(left, right):
    return (left.astype(FULL) + right.astype(FULL)).astype(LOW)


def gather_shards(block):
    for bit in reversed(range(bits_of(lax.axis_size("shard")))):
        block = jnp.concatenate([block, swap(block, "shard", bit)], axis=0)
    return block


def scatter_shards(blocks):
    for bit in range(bits_of(lax.axis_size("shard"))):
        half = blocks.shape[0] // 2
        blocks = add_low(blocks[:half], swap(blocks[half:], "shard", bit))
    return blocks[0]


def sum_replicas(block, first_bit):
    for bit in range(first_bit, bits_of(lax.axis_size("rep"))):
        block = add_low(block, swap(block, "rep", bit))
    return block


def bucket_onehot(period, buckets):
    index = np.arange(period)
    relative = np.where(index < period // 2, index, index - period)
    distance = np.abs(relative)
    bucket = buckets // 2 * (relative > 0).astype(np.int64)
    for border in BORDERS:
        bucket = bucket + (distance >= border).astype(np.int64)
    return (bucket[:, None] == np.arange(buckets)[None, :]).astype(np.float32)


def mm(left, right):
    return lax.dot_general(left, right, (((1,), (0,)), ((), ())), preferred_element_type=FULL)


def mm_nt(left, right):
    return lax.dot_general(left, right, (((1,), (1,)), ((), ())), preferred_element_type=FULL)


def mm_tn(left, right):
    return lax.dot_general(left, right, (((0,), (0,)), ((), ())), preferred_element_type=FULL)


def inverse_rms(values):
    return lax.rsqrt(jnp.mean(values * values, axis=-1, keepdims=True) + EPSILON)


def norm_back(values, scale, gain, grad):
    inner = jnp.mean(gain * grad * values, axis=-1, keepdims=True)
    return scale * gain * grad - values * (scale * scale * scale * inner)


def pick(mask, left, right):
    return jnp.where(mask, left.astype(FULL), right.astype(FULL)).astype(left.dtype)


def aligned(index, size):
    return pl.ds(pl.multiple_of(index, 8), size)


def lanes_at(index, size):
    return pl.ds(pl.multiple_of(index, LANES), size)


def bias_tiles(bias_row, rows):
    rolled = pltpu.roll(
        jnp.broadcast_to(bias_row, (rows, 2 * rows)), 0, 1, stride=1, stride_axis=0
    )
    return rolled[:, :rows], rolled[:, rows:]


def place_halves(pos, core, mine, other, full, shard_rows, shards):
    width = mine.shape[1]

    def place(j, carry):
        source = aligned(pos[j] * shard_rows, shard_rows)
        target = aligned(j * shard_rows, shard_rows)
        full[target, lanes_at(core * width, width)] = mine[source, :]
        full[target, lanes_at((1 - core) * width, width)] = other[source, :]
        return carry

    lax.fori_loop(0, shards, place, 0)


def attend_kernel(
    shards,
    heads_count,
    pos,
    meta,
    before,
    own,
    after,
    gain,
    mine,
    other,
    own_col,
    own_row,
    before_row,
    after_row,
    bias,
    heads,
    normed,
    qkv,
    weights,
    kv_before,
):
    rows, width = own.shape
    place_halves(pos, meta[0], mine, other, weights, width // shards, shards)

    def normed_of(ref):
        values = ref[...].astype(FULL)
        return (values * inverse_rms(values) * gain[...]).astype(LOW)

    normed[:rows, :] = normed_of(own)
    normed[rows:, :] = normed_of(after)
    normed_before = normed_of(before)
    hidden = weights.shape[1] // 3
    for part in range(3):
        columns = slice(part * hidden, (part + 1) * hidden)
        qkv[:, columns] = mm(normed[...], weights[:, columns]).astype(LOW)
        if part:
            kv_before[:, (part - 1) * hidden : part * hidden] = mm(
                normed_before, weights[:, columns]
            ).astype(LOW)
    in_own = own_col[...] == own_row[...]
    in_before = own_col[...] == before_row[...]
    in_after = own_col[...] == after_row[...]
    allowed = in_own | in_before | in_after
    size = hidden // heads_count
    for pair in range(heads_count // 2):
        mixed = []
        for head in (2 * pair, 2 * pair + 1):
            at = head * size
            query = qkv[:rows, at : at + size]
            keys = slice(hidden + at, hidden + at + size)
            values = slice(2 * hidden + at, 2 * hidden + at + size)
            near, far = bias_tiles(bias[head : head + 1, :], rows)
            scores = jnp.where(
                in_own,
                mm_nt(query, qkv[:rows, keys]) + near,
                jnp.where(
                    in_before,
                    mm_nt(query, kv_before[:, at : at + size]),
                    mm_nt(query, qkv[rows:, keys]),
                )
                + far,
            )
            scores = jnp.where(allowed, scores, NEG_FILL)
            expd = jnp.exp(scores - jnp.max(scores, axis=-1, keepdims=True))
            probs = expd * (1.0 / jnp.sum(expd, axis=-1, keepdims=True))
            total = mm(jnp.where(in_own, probs, 0.0).astype(LOW), qkv[:rows, values])
            total = total + mm(
                jnp.where(in_before, probs, 0.0).astype(LOW),
                kv_before[:, hidden + at : hidden + at + size],
            )
            total = total + mm(
                jnp.where(in_after, probs, 0.0).astype(LOW), qkv[rows:, values]
            )
            mixed.append(total)
        heads[:, 2 * pair * size : (2 * pair + 2) * size] = jnp.concatenate(mixed, axis=1).astype(LOW)


def feed_kernel(
    shards,
    pos,
    meta,
    heads,
    own,
    cotangent,
    gain,
    out_mine,
    out_other,
    part_0,
    part_1,
    part_2,
    part_3,
    output,
    d_resid,
    d_heads,
    normed_ff,
    hidden,
    d_gate,
    d_linear,
    d_gain,
    w_out,
    w_gate,
    w_up,
    w_down,
):
    rows, width = own.shape
    inner = w_gate.shape[1]
    shard_rows, down_rows = width // shards, inner // shards // PARTS
    slab = inner // PARTS
    tiles, down_tiles = slab // LANES, width // LANES
    block = part_0.shape[0] // shards
    place_halves(pos, meta[0], out_mine, out_other, w_out, shard_rows, shards)

    def place(j, carry):
        for relative, part in enumerate((part_0, part_1, part_2, part_3)):
            quarter = meta[1] ^ relative
            start = pos[j] * block
            target = aligned(j * shard_rows, shard_rows)
            for t in range(tiles):
                lane = lanes_at(quarter * slab + t * LANES, LANES)
                w_gate[target, lane] = part[aligned(start + t * shard_rows, shard_rows), :]
                w_up[target, lane] = part[aligned(start + (tiles + t) * shard_rows, shard_rows), :]
            down = start + 2 * tiles * shard_rows
            target = aligned(j * (PARTS * down_rows) + quarter * down_rows, down_rows)
            for t in range(down_tiles):
                w_down[target, t * LANES : (t + 1) * LANES] = part[
                    aligned(down + t * down_rows, down_rows), :
                ]
        return carry

    lax.fori_loop(0, shards, place, 0)
    resid = own[...].astype(FULL) + mm(heads[...], w_out[...])
    scale = inverse_rms(resid)
    normed_ff[...] = (resid * scale * gain[...]).astype(LOW)
    d_resid[...] = resid
    total = resid
    d_normed = jnp.zeros((rows, width), FULL)
    for q in range(PARTS):
        columns = slice(q * slab, (q + 1) * slab)
        gate = mm(normed_ff[...], w_gate[:, columns])
        linear = mm(normed_ff[...], w_up[:, columns])
        d_hidden = mm_nt(cotangent[...], w_down[columns, :])
        square = gate * gate
        tanh = jnp.tanh(GELU_A * (gate + GELU_B * square * gate))
        half = 0.5 * (1.0 + tanh)
        gelu = gate * half
        slope = half + 0.5 * gate * (1.0 - tanh * tanh) * (GELU_A * (1.0 + 3.0 * GELU_B * square))
        hidden[:, columns] = (gelu * linear).astype(LOW)
        d_gate[:, columns] = (d_hidden * linear * slope).astype(LOW)
        d_linear[:, columns] = (d_hidden * gelu).astype(LOW)
        total = total + mm(hidden[:, columns], w_down[columns, :])
        d_normed = d_normed + mm_nt(d_gate[:, columns], w_gate[:, columns])
        d_normed = d_normed + mm_nt(d_linear[:, columns], w_up[:, columns])
    output[...] = total.astype(LOW)
    resid = d_resid[...]
    d_gain[...] = jnp.sum(d_normed * resid * scale, axis=0, keepdims=True)
    grad = cotangent[...].astype(FULL) + norm_back(resid, scale, gain[...], d_normed)
    d_resid[...] = grad
    d_heads[...] = mm_nt(grad.astype(LOW), w_out[...]).astype(LOW)


def feed_grads_kernel(
    shards,
    pos,
    meta,
    heads,
    d_resid,
    normed_ff,
    hidden,
    d_gate,
    d_linear,
    cotangent,
    d_ff,
    d_out,
):
    width, inner = heads.shape[1], hidden.shape[1]
    shard_rows, down_rows = width // shards, inner // shards // PARTS
    slab = inner // PARTS
    tiles, down_tiles = slab // LANES, width // LANES
    for q in range(PARTS):
        columns = slice(q * slab, (q + 1) * slab)
        at = meta[2 + q]
        for side, grad in enumerate((d_gate, d_linear)):
            value = mm_tn(normed_ff[...], grad[:, columns]).astype(LOW)
            for j in range(shards):
                for t in range(tiles):
                    first = (side * tiles + t) * shard_rows
                    d_ff[at, pos[j], first : first + shard_rows, :] = value[
                        j * shard_rows : (j + 1) * shard_rows, t * LANES : (t + 1) * LANES
                    ]
        value = mm_tn(hidden[:, columns], cotangent[...]).astype(LOW)
        for piece in range(slab // down_rows):
            j, quarter = divmod(q * (slab // down_rows) + piece, PARTS)
            for t in range(down_tiles):
                first = 2 * tiles * shard_rows + t * down_rows
                d_ff[meta[2 + quarter], pos[j], first : first + down_rows, :] = value[
                    piece * down_rows : (piece + 1) * down_rows, t * LANES : (t + 1) * LANES
                ]
    half = width // 2
    grad = d_resid[...].astype(LOW)
    for side in range(2):
        value = mm_tn(heads[...], grad[:, side * half : (side + 1) * half]).astype(LOW)
        at = meta[0] ^ side
        for j in range(shards):
            d_out[at, pos[j], :, :] = value[j * shard_rows : (j + 1) * shard_rows, :]


def attend_grads_kernel(
    shards,
    first,
    last,
    size,
    pos,
    meta,
    qkv,
    normed,
    dh_own,
    dh_after,
    own_col,
    own_row,
    after_col,
    after_row,
    bias,
    d_cols,
    d_weights,
    d_bias,
    qkv_mix,
    dh_keep,
    dh_mix,
):
    rows, width = dh_own.shape
    hidden = width
    group = (last - first) * size
    tail = meta[6]
    is_last_col, is_last_row = own_col[...] == tail, own_row[...] == tail
    mix_col = jnp.where(is_last_col, own_col[...], after_col[...])
    mix_row = jnp.where(is_last_row, own_row[...], after_row[...])
    inside = (own_col[...] == own_row[...]) & jnp.logical_not(is_last_col)
    crossing = (mix_col == tail) & (mix_row == tail)
    turned = is_last_col != is_last_row
    began = (own_col[...] >= meta[7]) & jnp.logical_not(is_last_col)
    span = slice(first * size, last * size)
    for part in range(3):
        columns = slice(part * hidden + first * size, part * hidden + last * size)
        qkv_mix[:, part * group : (part + 1) * group] = pick(
            is_last_col, qkv[:rows, columns], qkv[rows:, columns]
        )
    keep = jnp.where(began, dh_own[:, span].astype(FULL), 0.0)
    dh_keep[...] = keep.astype(LOW)
    mixed = jnp.where(is_last_col, dh_own[:, span].astype(FULL), dh_after[:, span].astype(FULL))
    dh_mix[...] = jnp.where(mix_col == tail, mixed, 0.0).astype(LOW)

    def tile(query, key, value, grad, offset, mask):
        scores = jnp.where(mask, mm_nt(query, key) + offset, NEG_FILL)
        expd = jnp.exp(scores - jnp.max(scores, axis=-1, keepdims=True))
        probs = expd * (1.0 / jnp.sum(expd, axis=-1, keepdims=True))
        d_probs = mm_nt(grad, value)
        weighted = jnp.sum(d_probs * probs, axis=-1, keepdims=True)
        d_scores = (probs * (d_probs - weighted)).astype(LOW)
        return (
            mm(d_scores, key),
            mm_tn(d_scores, query),
            mm_tn(probs.astype(LOW), grad),
            d_scores.astype(FULL),
        )

    for pair in range((last - first) // 2):
        outs = []
        for index in (2 * pair, 2 * pair + 1):
            head = first + index
            near, far = bias_tiles(bias[head : head + 1, :], rows)
            at, here = head * size, index * size
            one = tile(
                qkv[:rows, at : at + size],
                qkv[:rows, hidden + at : hidden + at + size],
                qkv[:rows, 2 * hidden + at : 2 * hidden + at + size],
                dh_keep[:, here : here + size],
                near,
                inside,
            )
            two = tile(
                qkv_mix[:, here : here + size],
                qkv_mix[:, group + here : group + here + size],
                qkv_mix[:, 2 * group + here : 2 * group + here + size],
                dh_mix[:, here : here + size],
                jnp.where(turned, far, near),
                crossing,
            )
            flat = jnp.concatenate(
                [one[3] + jnp.where(turned, 0.0, two[3]), jnp.where(turned, two[3], 0.0)], axis=1
            )
            folded = flat[:8, :]
            for base in range(8, rows, 8):
                folded = folded + pltpu.roll(flat[base : base + 8, :], 2 * rows - base, 1)
            d_bias[8 * index : 8 * index + 8, :] = folded
            outs.append((one, two))
        for part in range(3):
            columns = slice(part * group + 2 * pair * size, part * group + (2 * pair + 2) * size)
            for side in range(2):
                d_cols[side * rows : (side + 1) * rows, columns] = jnp.concatenate(
                    [outs[0][side][part], outs[1][side][part]], axis=1
                ).astype(LOW)
    normed_mix = pick(is_last_col, normed[:rows, :], normed[rows:, :])
    half = 3 * group // 2
    shard_rows = width // shards
    for side in range(2):
        columns = slice(side * half, (side + 1) * half)
        value = mm_tn(normed[:rows, :], d_cols[:rows, columns])
        value = (value + mm_tn(normed_mix, d_cols[rows:, columns])).astype(LOW)
        at = meta[0] ^ side
        for j in range(shards):
            d_weights[at, pos[j], :, :] = value[j * shard_rows : (j + 1) * shard_rows, :]


def token_grads_kernel(
    sizes, meta, weights, own, after, gain, own_col, *refs
):
    *columns, d_own, d_after, d_gain = refs
    rows, width = own.shape
    is_last = own_col[...] == meta[6]
    total = jnp.zeros((2 * rows, width), FULL)
    begin = 0
    for ref, group in zip(columns, sizes, strict=True):
        for part in range(3):
            total = total + mm_nt(
                ref[:, part * group : (part + 1) * group],
                weights[:, part * width + begin : part * width + begin + group],
            )
        begin += group
    mine = jnp.where(is_last, total[rows:], total[:rows])
    sent = jnp.where(is_last, 0.0, total[rows:])
    d_own[...] = mine
    d_after[...] = sent.astype(LOW)
    values, ahead = own[...].astype(FULL), after[...].astype(FULL)
    share = mine * values * inverse_rms(values) + sent * ahead * inverse_rms(ahead)
    d_gain[...] = jnp.sum(share, axis=0, keepdims=True)


def tokens_kernel(own, gain, d_resid, d_own, d_before, d_tokens):
    values = own[...].astype(FULL)
    grad = d_own[...] + d_before[...].astype(FULL)
    d_tokens[...] = d_resid[...] + norm_back(values, inverse_rms(values), gain[...], grad)


def unpack_ff_kernel(meta, part_0, part_1, part_2, part_3, d_gate, d_up, d_down):
    shard_rows = d_gate.shape[0]
    slab = d_gate.shape[1] // PARTS
    down_rows, down_tiles = d_down.shape[0] // PARTS, d_down.shape[1] // LANES
    tiles = slab // LANES
    for relative, part in enumerate((part_0, part_1, part_2, part_3)):
        quarter = meta[1] ^ relative
        for t in range(tiles):
            lane = lanes_at(quarter * slab + t * LANES, LANES)
            d_gate[:, lane] = part[t * shard_rows : (t + 1) * shard_rows, :].astype(FULL)
            first = (tiles + t) * shard_rows
            d_up[:, lane] = part[first : first + shard_rows, :].astype(FULL)
        for t in range(down_tiles):
            first = 2 * tiles * shard_rows + t * down_rows
            d_down[aligned(quarter * down_rows, down_rows), t * LANES : (t + 1) * LANES] = part[
                first : first + down_rows, :
            ].astype(FULL)


def unpack_attend_kernel(sizes, meta, *refs):
    halves, (d_query, d_key, d_value) = refs[:-3], refs[-3:]
    begin = 0
    for g, group in enumerate(sizes):
        mine, other = halves[2 * g], halves[2 * g + 1]
        for core in range(2):

            @pl.when(meta[0] == core)
            def _():
                pair = (mine, other) if core == 0 else (other, mine)
                whole = jnp.concatenate([pair[0][...], pair[1][...]], axis=1).astype(FULL)
                for part, ref in enumerate((d_query, d_key, d_value)):
                    ref[:, begin : begin + group] = whole[:, part * group : (part + 1) * group]

        begin += group


def unpack_out_kernel(meta, mine, other, d_out):
    width = mine.shape[1]
    d_out[:, lanes_at(meta[0] * width, width)] = mine[...].astype(FULL)
    d_out[:, lanes_at((1 - meta[0]) * width, width)] = other[...].astype(FULL)


def call(kernel, scalars, arrays, outs, scratch=(), flops=0):
    def in_vmem(_):
        return pl.BlockSpec(memory_space=pltpu.VMEM)

    def in_smem(_):
        return pl.BlockSpec(memory_space=pltpu.SMEM)

    moved = sum(a.size * a.dtype.itemsize for a in (*arrays, *outs))
    return pl.pallas_call(
        kernel,
        out_shape=outs,
        in_specs=[in_smem(a) for a in scalars] + [in_vmem(a) for a in arrays],
        out_specs=tuple(in_vmem(a) for a in outs),
        scratch_shapes=scratch,
        compiler_params=pltpu.CompilerParams(vmem_limit_bytes=58 * 2**20),
        cost_estimate=pl.CostEstimate(flops=flops, bytes_accessed=moved, transcendentals=0),
    )(*scalars, *arrays)


def shaped(shape, dtype):
    return jax.ShapeDtypeStruct(shape, dtype)


def per_device(
    tokens,
    cotangent,
    offsets,
    w_query,
    w_key,
    w_value,
    w_attn_out,
    w_gate,
    w_up,
    w_ff_out,
    gain_attn,
    gain_ff,
    rel_table,
):
    rows, width = tokens.shape
    shards, reps = lax.axis_size("shard"), lax.axis_size("rep")
    shard, rep = lax.axis_index("shard"), lax.axis_index("rep")
    block_index = rep * shards + shard
    core, quarter = rep % 2, rep % PARTS
    heads_count, table_rows = rel_table.shape[1], rel_table.shape[0]
    buckets = table_rows * shards
    shard_rows, inner = w_gate.shape
    down_rows = w_ff_out.shape[0] // PARTS
    slab = inner // PARTS
    size = width // heads_count

    relative = jnp.arange(shards, dtype=jnp.int32) ^ shard
    pos = jnp.zeros_like(relative)
    for bit in range(bits_of(shards)):
        pos = pos | (((relative >> bit) & 1) << (bits_of(shards) - 1 - bit))
    quarters = jnp.arange(PARTS, dtype=jnp.int32) ^ quarter
    quarter_pos = ((quarters & 1) << 1) | (quarters >> 1)

    starts_all = jnp.arange(offsets.shape[0], dtype=jnp.int32) - offsets
    start_pad = jnp.pad(starts_all, (rows, rows), constant_values=-1)
    window = lax.dynamic_slice_in_dim(start_pad, block_index * rows, 3 * rows)
    before_row = window[:rows].reshape(1, rows)
    own_row = window[rows : 2 * rows].reshape(1, rows)
    after_row = window[2 * rows :].reshape(1, rows)
    own_col, after_col = own_row.reshape(rows, 1), after_row.reshape(rows, 1)
    meta = jnp.concatenate(
        [
            jnp.stack([core, quarter]),
            quarter_pos,
            jnp.stack([window[2 * rows - 1], block_index * rows]),
        ]
    ).astype(jnp.int32)

    qkv_own = jnp.concatenate([w_query, w_key, w_value], axis=1)
    qkv_half = lax.dynamic_slice_in_dim(qkv_own, core * (3 * width // 2), 3 * width // 2, axis=1)
    small = jnp.stack(
        [
            jnp.pad(gain_attn, (0, LANES - shard_rows)),
            jnp.pad(gain_ff, (0, LANES - shard_rows)),
            jnp.pad(rel_table.reshape(-1), (0, LANES - table_rows * heads_count)),
        ]
    )
    small = jnp.pad(small, ((0, 5), (0, 0)))
    up = [(i, i + 1) for i in range(shards - 1)]
    down = [(i + 1, i) for i in range(shards - 1)]
    small_all = gather_shards(small)
    qkv_mine = gather_shards(qkv_half)
    qkv_other = swap(qkv_mine, "rep", 0)
    before = lax.ppermute(tokens, "shard", up)
    after = lax.ppermute(tokens, "shard", down)
    out_half = lax.dynamic_slice_in_dim(w_attn_out, core * (width // 2), width // 2, axis=1)
    out_mine = gather_shards(out_half)
    out_other = swap(out_mine, "rep", 0)

    def tiles_of(matrix):
        count = matrix.shape[1] // LANES
        return [matrix[:, t * LANES : (t + 1) * LANES] for t in range(count)]

    ff_own = jnp.concatenate(
        tiles_of(lax.dynamic_slice_in_dim(w_gate, quarter * slab, slab, axis=1))
        + tiles_of(lax.dynamic_slice_in_dim(w_up, quarter * slab, slab, axis=1))
        + tiles_of(lax.dynamic_slice_in_dim(w_ff_out, quarter * down_rows, down_rows, axis=0)),
        axis=0,
    )
    ff_0 = gather_shards(ff_own)
    ff_2 = swap(ff_0, "rep", 1)
    ff_1 = swap(ff_0, "rep", 0)
    ff_3 = swap(ff_2, "rep", 0)

    order = (pos[:, None] == jnp.arange(shards, dtype=jnp.int32)[None, :]).astype(LOW)
    small_all = jnp.dot(
        order, small_all.reshape(shards, 8 * LANES), preferred_element_type=FULL
    ).reshape(shards, 8, LANES)
    gain_one = small_all[:, 0, :shard_rows].reshape(1, width)
    gain_two = small_all[:, 1, :shard_rows].reshape(1, width)
    table = small_all[:, 2, : table_rows * heads_count].reshape(buckets, heads_count)
    selector = jnp.asarray(bucket_onehot(2 * rows, buckets))
    bias = lax.dot_general(
        table.astype(LOW),
        selector.astype(LOW),
        (((0,), (1,)), ((), ())),
        preferred_element_type=FULL,
    )

    heads, normed, qkv, w_qkv = call(
        functools.partial(attend_kernel, shards, heads_count),
        (pos, meta),
        (
            before,
            tokens,
            after,
            gain_one,
            qkv_mine,
            qkv_other,
            own_col,
            own_row,
            before_row,
            after_row,
            bias,
        ),
        (
            shaped((rows, width), LOW),
            shaped((2 * rows, width), LOW),
            shaped((2 * rows, 3 * width), LOW),
            shaped((width, 3 * width), LOW),
        ),
        [pltpu.VMEM((rows, 2 * width), LOW)],
        flops=10 * rows * width * width * 2,
    )
    wide = shaped((rows, inner), LOW)
    output, d_resid, d_heads, normed_ff, hidden, d_gate, d_linear, d_gain_two = call(
        functools.partial(feed_kernel, shards),
        (pos, meta),
        (heads, tokens, cotangent, gain_two, out_mine, out_other, ff_0, ff_1, ff_2, ff_3),
        (
            shaped((rows, width), LOW),
            shaped((rows, width), FULL),
            shaped((rows, width), LOW),
            shaped((rows, width), LOW),
            wide,
            wide,
            wide,
            shaped((1, width), FULL),
        ),
        [
            pltpu.VMEM((width, width), LOW),
            pltpu.VMEM((width, inner), LOW),
            pltpu.VMEM((width, inner), LOW),
            pltpu.VMEM((inner, width), LOW),
        ],
        flops=14 * rows * width * inner,
    )
    d_heads_after = lax.ppermute(d_heads, "shard", down)
    block = ff_own.shape[0]
    d_ff, d_out = call(
        functools.partial(feed_grads_kernel, shards),
        (pos, meta),
        (heads, d_resid, normed_ff, hidden, d_gate, d_linear, cotangent),
        (
            shaped((PARTS, shards, block, LANES), LOW),
            shaped((2, shards, shard_rows, width // 2), LOW),
        ),
        flops=7 * rows * width * inner,
    )

    d_ff = add_low(d_ff[:2], swap(d_ff[2:], "rep", 0))
    d_ff = add_low(d_ff[0], swap(d_ff[1], "rep", 1))
    d_ff = sum_replicas(scatter_shards(d_ff), 2)
    d_ff_2 = swap(d_ff, "rep", 1)
    d_ff_1 = swap(d_ff, "rep", 0)
    d_ff_3 = swap(d_ff_2, "rep", 0)
    d_out = sum_replicas(scatter_shards(add_low(d_out[0], swap(d_out[1], "rep", 0))), 1)
    d_out_other = swap(d_out, "rep", 0)

    halves, column_grads, d_biases, sizes = [], [], [], []
    first = 0
    for count in GROUPS:
        group = count * size
        sizes.append(group)
        d_cols, d_weights, d_bias = call(
            functools.partial(attend_grads_kernel, shards, first, first + count, size),
            (pos, meta),
            (
                qkv,
                normed,
                d_heads,
                d_heads_after,
                own_col,
                own_row,
                after_col,
                after_row,
                bias,
            ),
            (
                shaped((2 * rows, 3 * group), LOW),
                shaped((2, shards, shard_rows, 3 * group // 2), LOW),
                shaped((8 * count, 2 * rows), FULL),
            ),
            [
                pltpu.VMEM((rows, 3 * group), LOW),
                pltpu.VMEM((rows, group), LOW),
                pltpu.VMEM((rows, group), LOW),
            ],
            flops=24 * rows * width * group,
        )
        first += count
        column_grads.append(d_cols)
        d_biases.append(d_bias)
        mine = add_low(d_weights[0], swap(d_weights[1], "rep", 0))
        mine = sum_replicas(scatter_shards(mine), 1)
        halves += [mine, swap(mine, "rep", 0)]

    d_own, d_after, d_gain_one = call(
        functools.partial(token_grads_kernel, tuple(sizes)),
        (meta,),
        (w_qkv, tokens, after, gain_one, own_col, *column_grads),
        (
            shaped((rows, width), FULL),
            shaped((rows, width), LOW),
            shaped((1, width), FULL),
        ),
        flops=12 * rows * width * width,
    )
    d_before = lax.ppermute(d_after, "shard", up)
    (d_tokens,) = call(
        tokens_kernel,
        (),
        (tokens, gain_one, d_resid, d_own, d_before),
        (shaped((rows, width), FULL),),
    )

    folds = np.stack([np.roll(bucket_onehot(2 * rows, buckets), row, axis=0) for row in range(8)])
    d_table = lax.dot_general(
        jnp.concatenate(d_biases, axis=0).reshape(heads_count, 16 * rows),
        jnp.asarray(folds.reshape(16 * rows, buckets)),
        (((1,), (0,)), ((), ())),
        precision=lax.Precision.HIGHEST,
    ).T
    smalls = jnp.concatenate([d_gain_one.reshape(-1), d_gain_two.reshape(-1), d_table.reshape(-1)])
    extra = -smalls.shape[0] % (8 * LANES)
    smalls = jnp.pad(smalls, (0, extra)).reshape(-1, LANES)
    for axis in ("rep", "shard"):
        for bit in range(bits_of(lax.axis_size(axis))):
            smalls = smalls + swap(smalls, axis, bit)
    smalls = smalls.reshape(-1)

    def own_part(begin, length):
        return lax.dynamic_slice_in_dim(smalls, begin + shard * length, length)

    d_w_gate, d_w_up, d_w_ff_out = call(
        unpack_ff_kernel,
        (meta,),
        (d_ff, d_ff_1, d_ff_2, d_ff_3),
        (
            shaped(w_gate.shape, FULL),
            shaped(w_up.shape, FULL),
            shaped(w_ff_out.shape, FULL),
        ),
    )
    (d_w_attn_out,) = call(
        unpack_out_kernel, (meta,), (d_out, d_out_other), (shaped(w_attn_out.shape, FULL),)
    )
    d_w_query, d_w_key, d_w_value = call(
        functools.partial(unpack_attend_kernel, tuple(sizes)),
        (meta,),
        tuple(halves),
        (shaped(w_query.shape, FULL),) * 3,
    )
    return (
        output,
        d_tokens,
        d_w_query,
        d_w_key,
        d_w_value,
        d_w_attn_out,
        d_w_gate,
        d_w_up,
        d_w_ff_out,
        own_part(0, shard_rows),
        own_part(width, shard_rows),
        own_part(2 * width, table_rows * heads_count).reshape(table_rows, heads_count),
    )


def solution(mesh):
    tokens_spec, rows_spec, line_spec = P(("rep", "shard"), None), P("shard", None), P("shard")
    return jax.shard_map(
        per_device,
        mesh=mesh,
        in_specs=(tokens_spec, tokens_spec, P()) + (rows_spec,) * 7 + (line_spec,) * 2 + (rows_spec,),
        out_specs=(tokens_spec,) * 2 + (rows_spec,) * 7 + (line_spec,) * 2 + (rows_spec,),
        check_vma=False,
    )
```

time: 1220 us -> 452 us (0.37)
  waiting for transfers between devices: 802 us -> 229 us
  matrix products: 178 us -> 2.42 us
  blocking collectives: 109 us -> 0 us
  Pallas kernels: 0 us -> 77.9 us
  starting transfers between devices: 11 us -> 66.4 us
  local copies, waits for them, and re-layouts: 82.9 us -> 52.5 us
  between operations: 16.4 us -> 1.65 us
    reduce_scatter x7 -> x0, waiting for transfers between devices: 527 us -> none  [the longest x1 121 us: per_device(): lax.psum_scatter(d_w_up, 'shard', scatter_dimension=0, tiled=True)]
    all_gather x7 -> x0, waiting for transfers between devices: 208 us -> none  [the longest x1 58.3 us: per_device(): lax.all_gather(w_up, 'shard', axis=0, tiled=True)]
    ppermute x4 -> x52, waiting for transfers between devices: 36.4 us -> 229 us  [the longest x48 211 us: swap(): return lax.ppermute(block, axis, [(i, i ^ 1 << bit) for i in range(count)])]
    dot_general x107 -> x3, matrix products: 178 us -> 2.42 us  [the longest x1 1.68 us: per_device(): lax.dot_general(table.astype(LOW), selector.astype(LOW), (((0,), (1,)), (...]
    pallas_call x0 -> x10, Pallas kernels: none -> 77.9 us  [call(): pl.pallas_call(kernel, out_shape=outs, in_specs=[in_smem(a) for a in scal...]
    unnamed x2 -> x0, blocking collectives: 58.4 us -> none
    ppermute x4 -> x52, starting transfers between devices: 9.94 us -> 66.4 us  [the longest x48 56.9 us: swap(): return lax.ppermute(block, axis, [(i, i ^ 1 << bit) for i in range(count)])]
    all_gather x1 -> x0, blocking collectives: 44.6 us -> none  [per_device(): lax.all_gather(rel_table, 'shard', axis=0, tiled=True)]
  transfers between devices with their start and end apart: 19 -> 52, of which waited for: 15 -> 21; matrix products, arithmetic and copies ran while one was open for 20% -> 7% of each run, Pallas kernels for 0% -> 11%
where the time goes in v1:
time: 452 us; the launch traced here: 447 us
  waiting for transfers between devices  229 us (51%)
  Pallas kernels  77.9 us (17%)
  starting transfers between devices  66.4 us (15%)
  local copies, waits for them, and re-layouts  52.5 us (12%)
  other arithmetic  17.9 us (4%)
    ppermute x48, waiting for transfers between devices, swap(): return lax.ppermute(block, axis, [(i, i ^ 1 << bit) for i in range(count)])  211 us
    pallas_call x10, Pallas kernels, call(): pl.pallas_call(kernel, out_shape=outs, in_specs=[in_smem(a) for a in scal...  77.9 us
    ppermute x48, starting transfers between devices, swap(): return lax.ppermute(block, axis, [(i, i ^ 1 << bit) for i in range(count)])  56.9 us
    unnamed x107, local copies, waits for them, and re-layouts  31.4 us
    convert_element_type x16, other arithmetic, add_low(): return (left.astype(FULL) + right.astype(FULL)).astype(LOW)  13.4 us
    ppermute x1, waiting for transfers between devices, per_device(): d_heads_after = lax.ppermute(d_heads, 'shard', down)  11.5 us
  transfers between devices with their start and end apart: 52, of which 21 were waited for; matrix products, arithmetic and copies ran while one was open for 7% of the time, Pallas kernels for 11%

profile of v1, /device:TPU:0, one launch (start us, length us, event | category | flops | bytes accessed | tf_op | source)
XLA Modules:
  0.0 447.3 jit_solution(4316618522873108988)
XLA Ops:
  28.4 11.5 %collective-permute-done.13 = bf16[1152,128]{1,0:T(8,128)(2,1)S(1)} collective-permute-done((bf16[1152,128]{1,0:T(8,128)(2,1)S(1)}, bf16[1152,128]{1,0:T(8,128)(2,1)S(1)}, u32[]{:S(2)}, u32[]{:S(2)}) %collective-permute-start.13) | collective-permute-done | bytes 294944 | tf_op jit(solution)/shard_map/ppermute | solution.py:29
  41.5 13.8 %collective-permute-done.14 = bf16[2304,128]{1,0:T(8,128)(2,1)S(1)} collective-permute-done((bf16[2304,128]{1,0:T(8,128)(2,1)S(1)}, bf16[2304,128]{1,0:T(8,128)(2,1)S(1)}, u32[]{:S(2)}, u32[]{:S(2)}) %collective-permute-start.14) | collective-permute-done | bytes 589856 | tf_op jit(solution)/shard_map/ppermute | solution.py:29
  57.5 25.0 %collective-permute-done.15 = bf16[4608,128]{1,0:T(8,128)(2,1)S(1)} collective-permute-done((bf16[4608,128]{1,0:T(8,128)(2,1)S(1)}, bf16[4608,128]{1,0:T(8,128)(2,1)S(1)}, u32[]{:S(2)}, u32[]{:S(2)}) %collective-permute-start.15) | collective-permute-done | bytes 1179680 | tf_op jit(solution)/shard_map/ppermute | solution.py:29
  89.5 8.6 %collective-permute-done.5 = bf16[96,1152]{1,0:T(8,128)(2,1)S(1)} collective-permute-done((bf16[96,1152]{1,0:T(8,128)(2,1)S(1)}, bf16[96,1152]{1,0:T(8,128)(2,1)S(1)}, u32[]{:S(2)}, u32[]{:S(2)}) %collective-permute-start.5) | collective-permute-done | bytes 221216 | tf_op jit(solution)/shard_map/ppermute | solution.py:29
  98.6 11.1 %collective-permute-done.6 = bf16[192,1152]{1,0:T(8,128)(2,1)S(1)} collective-permute-done((bf16[192,1152]{1,0:T(8,128)(2,1)S(1)}, bf16[192,1152]{1,0:T(8,128)(2,1)S(1)}, u32[]{:S(2)}, u32[]{:S(2)}) %collective-permute-start.6) | collective-permute-done | bytes 442400 | tf_op jit(solution)/shard_map/ppermute | solution.py:29
  114.7 19.9 %collective-permute-done.17.part_2 = bf16[9216,128]{1,0:T(8,128)(2,1)} collective-permute-done((bf16[9216,128]{1,0:T(8,128)(2,1)}, bf16[9216,128]{1,0:T(8,128)(2,1)}, u32[]{:S(2)}, u32[]{:S(2)}) %collective-permute-start.17) | collective-permute-done | bytes 2359328 | tf_op jit(solution)/shard_map/ppermute | solution.py:29
  148.4 6.5 %collective-permute-done.4 = bf16[32,128]{1,0:T(8,128)(2,1)S(1)} collective-permute-done((bf16[32,128]{1,0:T(8,128)(2,1)S(1)}, bf16[32,128]{1,0:T(8,128)(2,1)S(1)}, u32[]{:S(2)}, u32[]{:S(2)}) %collective-permute-start.4) | collective-permute-done | bytes 8224 | tf_op jit(solution)/shard_map/ppermute | solution.py:29
  157.6 6.0 %collective-permute-done.11 = bf16[384,384]{1,0:T(8,128)(2,1)S(1)} collective-permute-done((bf16[384,384]{1,0:T(8,128)(2,1)S(1)}, bf16[384,384]{1,0:T(8,128)(2,1)S(1)}, u32[]{:S(2)}, u32[]{:S(2)}) %collective-permute-start.11) | collective-permute-done | bytes 294944 | tf_op jit(solution)/shard_map/ppermute | solution.py:29
  170.0 5.6 %collective-permute-done.1.after = bf16[256,768]{1,0:T(8,128)(2,1)S(1)} collective-permute-done((bf16[256,768]{1,0:T(8,128)(2,1)S(1)}, bf16[256,768]{1,0:T(8,128)(2,1)S(1)}, u32[]{:S(2)}, u32[]{:S(2)}) %collective-permute-start.1) | collective-permute-done | bytes 393248 | tf_op jit(solution)/shard_map/ppermute | solution.py:592
  176.4 12.9 %shard_map.238 = (bf16[256,768]{1,0:T(8,128)(2,1)}, bf16[512,768]{1,0:T(8,128)(2,1)}, bf16[512,2304]{1,0:T(8,128)(2,1)}, bf16[768,2304]{1,0:T(8,128)(2,1)}) custom-call(s32[8]{0:T(128)} %copy-done.37, s32[8]{0:T(128)} %concatenate.60.meta, bf16[256,768]{1,0:T(8,128)(2,1)} %collective-permute-done.before, bf16[256,768]{1,0:T(8,128)(2,1)} %own.7, ...), custom_call_target="tpu_custom_call" | custom-call | flops 3019898880 | bytes 11828224 | tf_op jit(solution)/shard_map/pallas_call | solution.py:512
  189.3 15.7 %shard_map.239 = (bf16[256,768]{1,0:T(8,128)(2,1)}, f32[256,768]{1,0:T(8,128)}, bf16[256,768]{1,0:T(8,128)(2,1)}, bf16[256,768]{1,0:T(8,128)(2,1)}, bf16[256,204...) custom-call(s32[8]{0:T(128)} %copy-done.37, s32[8]{0:T(128)} %concatenate.60.meta, ...), custom_call_target="tpu_custom_call" | custom-call | flops 5637144576 | bytes 16914432 | tf_op jit(solution)/shard_map/pallas_call | solution.py:512
  205.0 9.4 %shard_map.245 = (bf16[4,8,1152,128]{3,2,1,0:T(8,128)(2,1)}, bf16[2,8,96,384]{3,2,1,0:T(8,128)(2,1)}) custom-call(s32[8]{0:T(128)} %copy-done.37, s32[8]{0:T(128)} %concatenate.60.meta, bf16[256,768]{1,0:T(8,128)(2,1)} %get-tuple-element.41.heads, f32[256,768]{1,0:T(8,128)} %get-tuple-element.43.d_resid, bf16[256,768]{1,0:T(8,128)(2,1)} %get-tuple-element.57.normed_ff, ...), custom_call_target="tpu_custom_call" | custom-call | flops 2818572288 | bytes 15728640 | tf_op jit(solution)/shard_map/pallas_call | solution.py:512
  214.3 5.0 %slice.212 = bf16[2,8,1152,128]{3,2,1,0:T(8,128)(2,1)} slice(bf16[4,8,1152,128]{3,2,1,0:T(8,128)(2,1)} %get-tuple-element.62), slice={[2:4], [0:8], [0:1152], [0:128]} | slice | bytes 9437184 | tf_op jit(solution)/shard_map/slice | solution.py:688
  221.8 11.5 %collective-permute-done.19.dh_after = bf16[256,768]{1,0:T(8,128)(2,1)S(1)} collective-permute-done((bf16[256,768]{1,0:T(8,128)(2,1)S(1)}, bf16[256,768]{1,0:T(8,128)(2,1)S(1)}, u32[]{:S(2)}, u32[]{:S(2)}) %collective-permute-start.19) | collective-permute-done | bytes 393248 | tf_op jit(solution)/shard_map/ppermute | solution.py:675
  234.1 9.1 %shard_map.241 = (bf16[512,768]{1,0:T(8,128)(2,1)}, bf16[2,8,96,384]{3,2,1,0:T(8,128)(2,1)}, f32[32,512]{1,0:T(8,128)}) custom-call(s32[8]{0:T(128)} %copy-done.37, s32[8]{0:T(128)} %concatenate.60.meta, bf16[512,2304]{1,0:T(8,128)(2,1)} %get-tuple-element.45.qkv, bf16[512,768]{1,0:T(8,128)(2,1)} %get-tuple-element.46.normed, ...), custom_call_target="tpu_custom_call" | custom-call | flops 1207959552 | bytes 5992448 | tf_op jit(solution)/shard_map/pallas_call | solution.py:512
  243.2 15.3 %shard_map.240 = (bf16[512,1536]{1,0:T(8,128)(2,1)}, bf16[2,8,96,768]{3,2,1,0:T(8,128)(2,1)}, f32[64,512]{1,0:T(8,128)}) custom-call(s32[8]{0:T(128)} %copy-done.37, s32[8]{0:T(128)} %concatenate.60.meta, bf16[512,2304]{1,0:T(8,128)(2,1)} %get-tuple-element.45.qkv, bf16[512,768]{1,0:T(8,128)(2,1)} %get-tuple-element.46.normed, ...), custom_call_target="tpu_custom_call" | custom-call | flops 2415919104 | bytes 8024064 | tf_op jit(solution)/shard_map/pallas_call | solution.py:512
  259.5 5.0 %add_convert_fusion = bf16[2,8,1152,128]{3,2,1,0:T(8,128)(2,1)S(1)} fusion(bf16[2,8,1152,128]{3,2,1,0:T(8,128)(2,1)} %collective-permute-done.39, bf16[4,8,1152,128]{3,2,1,0:T(8,128)(2,1)} %get-tuple-element.62), kind=kLoop, calls=%fused_computation | loop fusion | flops 9437184 | bytes 14155776 | tf_op jit(solution)/shard_map/convert_element_type | solution.py:33
  269.6 6.1 %shard_map.242 = (f32[256,768]{1,0:T(8,128)}, bf16[256,768]{1,0:T(8,128)(2,1)}, f32[1,768]{1,0:T(1,128)}) custom-call(s32[8]{0:T(128)} %concatenate.60.meta, bf16[768,2304]{1,0:T(8,128)(2,1)} %get-tuple-element.44.weights, bf16[256,768]{1,0:T(8,128)(2,1)} %own.7, bf16[256,768]{1,0:T(8,128)(2,1)} %copy-done.13, f32[1,768]{1,0:T(1,128)} %reshape_squeeze.7.gain, ...), custom_call_target="tpu_custom_call" | custom-call | flops 1811939328 | bytes 7871488 | tf_op jit(solution)/shard_map/pallas_call | solution.py:512
  278.8 42.1 %collective-permute-done.48 = f32[16,128]{1,0:T(8,128)S(1)} collective-permute-done((f32[16,128]{1,0:T(8,128)S(1)}, f32[16,128]{1,0:T(8,128)S(1)}, u32[]{:S(2)}, u32[]{:S(2)}) %collective-permute-start.48) | collective-permute-done | bytes 8224 | tf_op jit(solution)/shard_map/ppermute | solution.py:29
  362.5 28.5 %collective-permute-done.22 = bf16[4,96,768]{2,1,0:T(8,128)(2,1)S(1)} collective-permute-done((bf16[4,96,768]{2,1,0:T(8,128)(2,1)S(1)}, bf16[4,96,768]{2,1,0:T(8,128)(2,1)S(1)}, u32[]{:S(2)}, u32[]{:S(2)}) %collective-permute-start.22) | collective-permute-done | bytes 589856 | tf_op jit(solution)/shard_map/ppermute | solution.py:29
  394.7 9.0 %collective-permute-done.23 = bf16[2,96,768]{2,1,0:T(8,128)(2,1)S(1)} collective-permute-done((bf16[2,96,768]{2,1,0:T(8,128)(2,1)S(1)}, bf16[2,96,768]{2,1,0:T(8,128)(2,1)S(1)}, u32[]{:S(2)}, u32[]{:S(2)}) %collective-permute-start.23) | collective-permute-done | bytes 294944 | tf_op jit(solution)/shard_map/ppermute | solution.py:29
  403.8 10.6 %collective-permute-done.42 = bf16[2,1152,128]{2,1,0:T(8,128)(2,1)S(1)} collective-permute-done((bf16[2,1152,128]{2,1,0:T(8,128)(2,1)S(1)}, bf16[2,1152,128]{2,1,0:T(8,128)(2,1)S(1)}, u32[]{:S(2)}, u32[]{:S(2)}) %collective-permute-start.42) | collective-permute-done | bytes 589856 | tf_op jit(solution)/shard_map/ppermute | solution.py:29
  419.4 5.9 %collective-permute-done.43 = bf16[1,1152,128]{2,1,0:T(8,128)(2,1)S(1)} collective-permute-done((bf16[1,1152,128]{2,1,0:T(8,128)(2,1)S(1)}, bf16[1,1152,128]{2,1,0:T(8,128)(2,1)S(1)}, u32[]{:S(2)}, u32[]{:S(2)}) %collective-permute-start.43) | collective-permute-done | bytes 294944 | tf_op jit(solution)/shard_map/ppermute | solution.py:29
  427.8 5.1 %collective-permute-done.31 = bf16[96,384]{1,0:T(8,128)(2,1)S(1)} collective-permute-done((bf16[96,384]{1,0:T(8,128)(2,1)S(1)}, bf16[96,384]{1,0:T(8,128)(2,1)S(1)}, u32[]{:S(2)}, u32[]{:S(2)}) %collective-permute-start.31) | collective-permute-done | bytes 73760 | tf_op jit(solution)/shard_map/ppermute | solution.py:29
  (283 shorter events, 146.5 us)
Async XLA Ops:
  22.6 17.4 %collective-permute-start.13 = (bf16[1152,128]{1,0:T(8,128)(2,1)S(1)}, bf16[1152,128]{1,0:T(8,128)(2,1)S(1)}, u32[]{:S(2)}, u32[]{:S(2)}) collective-permute-start(bf16[1152,128]{1,0:T(8,128)(2,1)S(1)} %get-tuple-element.104), channel_id=1, source_target_pairs={{0,4},{1,5},{2,6},{3,7},{4,0},{5,1},{6,2},{7,3},{8,12},{9,13},{10,... | collective-permute-start | bytes 884744 | tf_op jit(solution)/shard_map/ppermute | solution.py:29
  56.2 26.3 %collective-permute-start.15 = (bf16[4608,128]{1,0:T(8,128)(2,1)S(1)}, bf16[4608,128]{1,0:T(8,128)(2,1)S(1)}, u32[]{:S(2)}, u32[]{:S(2)}) collective-permute-start(bf16[4608,128]{1,0:T(8,128)(2,1)S(1)} %get-tuple-element.70), channel_id=1, source_target_pairs={{0,1},{1,0},{2,3},{3,2},{4,5},{5,4},{6,7},{7,6},{8,9},{9,8},{10,11... | collective-permute-start | bytes 3538952 | tf_op jit(solution)/shard_map/ppermute | solution.py:29
  83.5 51.0 %collective-permute-start.17 = (bf16[9216,128]{1,0:T(8,128)(2,1)}, bf16[9216,128]{1,0:T(8,128)(2,1)}, u32[]{:S(2)}, u32[]{:S(2)}) collective-permute-start(bf16[9216,128]{1,0:T(8,128)(2,1)} %constant_dynamic-update-slice_fusion.45.part_0), channel_id=1, source_target_pairs={{0,16},{8,24},{16,0},{24,8},{1,17},{9,25},{17,1},{25,9},{2,18},{10... | collective-permute-start | bytes 7077896 | tf_op jit(solution)/shard_map/ppermute | solution.py:29
  109.7 24.8 %collective-permute-start.7 = (bf16[384,1152]{1,0:T(8,128)(2,1)S(1)}, bf16[384,1152]{1,0:T(8,128)(2,1)}, u32[]{:S(2)}, u32[]{:S(2)}) collective-permute-start(bf16[384,1152]{1,0:T(8,128)(2,1)S(1)} %pad_maximum_fusion.1), channel_id=1, source_target_pairs={{0,1},{1,0},{2,3},{3,2},{4,5},{5,4},{6,7},{7,6},{8,9},{9,8},{10,11... | collective-permute-start | bytes 2654216 | tf_op jit(solution)/shard_map/ppermute | solution.py:29
  111.5 25.6 %collective-permute-start.2 = (bf16[8,128]{1,0:T(8,128)(2,1)S(1)}, bf16[8,128]{1,0:T(8,128)(2,1)S(1)}, u32[]{:S(2)}, u32[]{:S(2)}) collective-permute-start(bf16[8,128]{1,0:T(8,128)(2,1)S(1)} %fusion.19), channel_id=1, source_target_pairs={{0,4},{1,5},{2,6},{3,7},{4,0},{5,1},{6,2},{7,3},{8,12},{9,13},{10,... | collective-permute-start | bytes 6152 | tf_op jit(solution)/shard_map/ppermute | solution.py:29
  113.6 26.6 %collective-permute-start.9 = (bf16[96,384]{1,0:T(8,128)(2,1)S(1)}, bf16[96,384]{1,0:T(8,128)(2,1)S(1)}, u32[]{:S(2)}, u32[]{:S(2)}) collective-permute-start(bf16[96,384]{1,0:T(8,128)(2,1)S(1)} %constant_dynamic-slice_fusion), channel_id=1, source_target_pairs={{0,4},{1,5},{2,6},{3,7},{4,0},{5,1},{6,2},{7,3},{8,12},{9,13},{10,... | collective-permute-start | bytes 221192 | tf_op jit(solution)/shard_map/ppermute | solution.py:29
  114.6 74.7 %collective-permute-start.16 = (bf16[9216,128]{1,0:T(8,128)(2,1)}, bf16[9216,128]{1,0:T(8,128)(2,1)}, u32[]{:S(2)}, u32[]{:S(2)}) collective-permute-start(bf16[9216,128]{1,0:T(8,128)(2,1)} %constant_dynamic-update-slice_fusion.45.part_0), channel_id=1, source_target_pairs={{0,8},{8,0},{16,24},{24,16},{1,9},{9,1},{17,25},{25,17},{2,10},{10... | collective-permute-start | bytes 7077896 | tf_op jit(solution)/shard_map/ppermute | solution.py:29
  134.5 54.8 %collective-permute-start.18 = (bf16[9216,128]{1,0:T(8,128)(2,1)}, bf16[9216,128]{1,0:T(8,128)(2,1)}, u32[]{:S(2)}, u32[]{:S(2)}) collective-permute-start(bf16[9216,128]{1,0:T(8,128)(2,1)} %collective-permute-done.17.part_2), channel_id=1, source_target_pairs={{0,8},{8,0},{16,24},{24,16},{1,9},{9,1},{17,25},{25,17},{2,10},{10... | collective-permute-start | bytes 7077896 | tf_op jit(solution)/shard_map/ppermute | solution.py:29
  135.9 39.7 %collective-permute-start.8 = (bf16[768,1152]{1,0:T(8,128)(2,1)S(1)}, bf16[768,1152]{1,0:T(8,128)(2,1)}, u32[]{:S(2)}, u32[]{:S(2)}) collective-permute-start(bf16[768,1152]{1,0:T(8,128)(2,1)S(1)} %pad_maximum_fusion.mine), channel_id=1, source_target_pairs={{0,8},{8,0},{16,24},{24,16},{1,9},{9,1},{17,25},{25,17},{2,10},{10... | collective-permute-start | bytes 5308424 | tf_op jit(solution)/shard_map/ppermute | solution.py:29
  142.9 23.9 %collective-permute-start = (bf16[256,768]{1,0:T(8,128)(2,1)S(1)}, bf16[256,768]{1,0:T(8,128)(2,1)}, u32[]{:S(2)}, u32[]{:S(2)}) collective-permute-start(bf16[256,768]{1,0:T(8,128)(2,1)S(1)} %copy-done.5), channel_id=1, source_target_pairs={{0,1},{1,2},{2,3},{3,4},{4,5},{5,6},{6,7},{8,9},{9,10},{10,11},{11... | collective-permute-start | bytes 1179656 | tf_op jit(solution)/shard_map/ppermute | solution.py:591
  166.8 22.5 %collective-permute-start.12 = (bf16[768,384]{1,0:T(8,128)(2,1)S(1)}, bf16[768,384]{1,0:T(8,128)(2,1)}, u32[]{:S(2)}, u32[]{:S(2)}) collective-permute-start(bf16[768,384]{1,0:T(8,128)(2,1)S(1)} %pad_maximum_fusion.2.out_mine), channel_id=1, source_target_pairs={{0,8},{8,0},{16,24},{24,16},{1,9},{9,1},{17,25},{25,17},{2,10},{10... | collective-permute-start | bytes 1769480 | tf_op jit(solution)/shard_map/ppermute | solution.py:29
  219.3 40.2 %collective-permute-start.39 = (bf16[2,8,1152,128]{3,2,1,0:T(8,128)(2,1)}, bf16[2,8,1152,128]{3,2,1,0:T(8,128)(2,1)}, u32[]{:S(2)}, u32[]{:S(2)}) collective-permute-start(bf16[2,8,1152,128]{3,2,1,0:T(8,128)(2,1)} %slice.212), channel_id=1, source_target_pairs={{0,8},{8,0},{16,24},{24,16},{1,9},{9,1},{17,25},{25,17},{2,10},{10... | collective-permute-start | bytes 14155784 | tf_op jit(solution)/shard_map/ppermute | solution.py:29
  267.5 80.5 %collective-permute-start.40 = (bf16[8,1152,128]{2,1,0:T(8,128)(2,1)}, bf16[8,1152,128]{2,1,0:T(8,128)(2,1)S(1)}, u32[]{:S(2)}, u32[]{:S(2)}) collective-permute-start(bf16[8,1152,128]{2,1,0:T(8,128)(2,1)} %slice_bitcast_fusion), channel_id=1, source_target_pairs={{0,16},{8,24},{16,0},{24,8},{1,17},{9,25},{17,1},{25,9},{2,18},{10... | collective-permute-start | bytes 7077896 | tf_op jit(solution)/shard_map/ppermute | solution.py:29
  277.6 55.0 %collective-permute-start.33 = (bf16[8,96,384]{2,1,0:T(8,128)(2,1)S(1)}, bf16[8,96,384]{2,1,0:T(8,128)(2,1)}, u32[]{:S(2)}, u32[]{:S(2)}) collective-permute-start(bf16[8,96,384]{2,1,0:T(8,128)(2,1)S(1)} %slice_bitcast_fusion.3), channel_id=1, source_target_pairs={{0,8},{8,0},{16,24},{24,16},{1,9},{9,1},{17,25},{25,17},{2,10},{10... | collective-permute-start | bytes 1769480 | tf_op jit(solution)/shard_map/ppermute | solution.py:29
  278.2 42.7 %collective-permute-start.48 = (f32[16,128]{1,0:T(8,128)S(1)}, f32[16,128]{1,0:T(8,128)S(1)}, u32[]{:S(2)}, u32[]{:S(2)}) collective-permute-start(f32[16,128]{1,0:T(8,128)S(1)} %fusion.30), channel_id=1, source_target_pairs={{0,16},{8,24},{16,0},{24,8},{1,17},{9,25},{17,1},{25,9},{2,18},{10... | collective-permute-start | bytes 24584 | tf_op jit(solution)/shard_map/ppermute | solution.py:29
  323.4 110.0 %collective-permute-start.20 = (bf16[256,768]{1,0:T(8,128)(2,1)}, bf16[256,768]{1,0:T(8,128)(2,1)S(1)}, u32[]{:S(2)}, u32[]{:S(2)}) collective-permute-start(bf16[256,768]{1,0:T(8,128)(2,1)} %get-tuple-element.51), channel_id=1, source_target_pairs={{0,1},{1,2},{2,3},{3,4},{4,5},{5,6},{6,7},{8,9},{9,10},{10,11},{11... | collective-permute-start | bytes 1179656 | tf_op jit(solution)/shard_map/ppermute | solution.py:746
  329.1 23.0 %collective-permute-start.21 = (bf16[8,96,768]{2,1,0:T(8,128)(2,1)}, bf16[8,96,768]{2,1,0:T(8,128)(2,1)}, u32[]{:S(2)}, u32[]{:S(2)}) collective-permute-start(bf16[8,96,768]{2,1,0:T(8,128)(2,1)} %slice_bitcast_fusion.2), channel_id=1, source_target_pairs={{0,8},{8,0},{16,24},{24,16},{1,9},{9,1},{17,25},{25,17},{2,10},{10... | collective-permute-start | bytes 3538952 | tf_op jit(solution)/shard_map/ppermute | solution.py:29
  350.3 41.3 %collective-permute-start.41 = (bf16[4,1152,128]{2,1,0:T(8,128)(2,1)S(1)}, bf16[4,1152,128]{2,1,0:T(8,128)(2,1)S(1)}, u32[]{:S(2)}, u32[]{:S(2)}) collective-permute-start(bf16[4,1152,128]{2,1,0:T(8,128)(2,1)S(1)} %slice.245), channel_id=1, source_target_pairs={{0,1},{1,0},{2,3},{3,2},{4,5},{5,4},{6,7},{7,6},{8,9},{9,8},{10,11... | collective-permute-start | bytes 3538952 | tf_op jit(solution)/shard_map/ppermute | solution.py:29
  353.7 37.3 %collective-permute-start.22 = (bf16[4,96,768]{2,1,0:T(8,128)(2,1)S(1)}, bf16[4,96,768]{2,1,0:T(8,128)(2,1)S(1)}, u32[]{:S(2)}, u32[]{:S(2)}) collective-permute-start(bf16[4,96,768]{2,1,0:T(8,128)(2,1)S(1)} %slice.225), channel_id=1, source_target_pairs={{0,1},{1,0},{2,3},{3,2},{4,5},{5,4},{6,7},{7,6},{8,9},{9,8},{10,11... | collective-permute-start | bytes 1769480 | tf_op jit(solution)/shard_map/ppermute | solution.py:29
  358.2 36.0 %collective-permute-start.28 = (bf16[4,96,384]{2,1,0:T(8,128)(2,1)S(1)}, bf16[4,96,384]{2,1,0:T(8,128)(2,1)S(1)}, u32[]{:S(2)}, u32[]{:S(2)}) collective-permute-start(bf16[4,96,384]{2,1,0:T(8,128)(2,1)S(1)} %slice.231), channel_id=1, source_target_pairs={{0,1},{1,0},{2,3},{3,2},{4,5},{5,4},{6,7},{7,6},{8,9},{9,8},{10,11... | collective-permute-start | bytes 884744 | tf_op jit(solution)/shard_map/ppermute | solution.py:29
  361.0 32.8 %collective-permute-start.37 = (bf16[96,384]{1,0:T(8,128)(2,1)S(1)}, bf16[96,384]{1,0:T(8,128)(2,1)S(1)}, u32[]{:S(2)}, u32[]{:S(2)}) collective-permute-start(bf16[96,384]{1,0:T(8,128)(2,1)S(1)} %fusion.9), channel_id=1, source_target_pairs={{0,16},{8,24},{16,0},{24,8},{1,17},{9,25},{17,1},{25,9},{2,18},{10... | collective-permute-start | bytes 221192 | tf_op jit(solution)/shard_map/ppermute | solution.py:29
  391.9 22.5 %collective-permute-start.42 = (bf16[2,1152,128]{2,1,0:T(8,128)(2,1)S(1)}, bf16[2,1152,128]{2,1,0:T(8,128)(2,1)S(1)}, u32[]{:S(2)}, u32[]{:S(2)}) collective-permute-start(bf16[2,1152,128]{2,1,0:T(8,128)(2,1)S(1)} %slice.247), channel_id=1, source_target_pairs={{0,2},{1,3},{2,0},{3,1},{4,6},{5,7},{6,4},{7,5},{8,10},{9,11},{10,... | collective-permute-start | bytes 1769480 | tf_op jit(solution)/shard_map/ppermute | solution.py:29
  393.8 43.3 %collective-permute-start.38 = (bf16[96,384]{1,0:T(8,128)(2,1)S(1)}, bf16[96,384]{1,0:T(8,128)(2,1)S(1)}, u32[]{:S(2)}, u32[]{:S(2)}) collective-permute-start(bf16[96,384]{1,0:T(8,128)(2,1)S(1)} %add_convert_fusion.12.mine), channel_id=1, source_target_pairs={{0,8},{8,0},{16,24},{24,16},{1,9},{9,1},{17,25},{25,17},{2,10},{10... | collective-permute-start | bytes 221192 | tf_op jit(solution)/shard_map/ppermute | solution.py:29
  394.3 21.7 %collective-permute-start.29 = (bf16[2,96,384]{2,1,0:T(8,128)(2,1)S(1)}, bf16[2,96,384]{2,1,0:T(8,128)(2,1)S(1)}, u32[]{:S(2)}, u32[]{:S(2)}) collective-permute-start(bf16[2,96,384]{2,1,0:T(8,128)(2,1)S(1)} %slice.233), channel_id=1, source_target_pairs={{0,2},{1,3},{2,0},{3,1},{4,6},{5,7},{6,4},{7,5},{8,10},{9,11},{10,... | collective-permute-start | bytes 442376 | tf_op jit(solution)/shard_map/ppermute | solution.py:29
  (66 other events, 908.4 us)
